TPU v7x, 256 devices: a whole 4x4x8 slice. The times are simulated.
256 devices in a mesh: traj: 32 (over z, y), seg: 8 (over x, core).
Axes of the slice: x: 4, y: 4, z: 8, core: 2. Of those that a mesh axis runs over, the one named last changes fastest.
Arguments:
- coords: float32 [32, 1024, 3, 512], P('traj', 'seg')
- pairs: int32 [2, 1024], replicated, may hold values from 0 to 511, as said below
- lengths: int32 [32], P('traj'), may hold values from 1 to 1024, 24576 in all
Outputs:
- projected: float32 [32, 1024, 128], P('traj', 'seg')
Inputs may be any that keep to these rules, and one draw needn't show every extreme that they name: `pairs`: atom indices; the two atoms of a contact differ. `lengths`: each trajectory's recorded frames fill its first slots.
All inputs are finite; a program needn't handle non-finite values. No bound on the sum of `lengths` on one device may be relied on, other than what follows from the above.
Results may differ from a plain program's by a relative error of at most 0.0003.
Values sent between devices are 32-bit elements; how exact they have to be, the bound alone decides.
No kernel may reach another device: no remote copies, remote signals or barrier semaphores. Data moves between devices by JAX's collectives and lax.ppermute only.
A program may use at most 128 MiB of HBM per device.

v0:
```python
import jax
import jax.numpy as jnp
from jax import lax
from jax.sharding import PartitionSpec as P

K = 128
LAG = 10
ITERS = 3
exact_mode = lax.Precision.HIGHEST
soft_square = 0.1
ridge_term = 0.01
spectral_shift = 2.0


def from_behind(x, axis, by):
    peers = lax.axis_size(axis)
    pairs = [(i, i + by) for i in range(peers) if 0 <= i + by < peers]
    return lax.ppermute(x, axis, pairs)


def featurize(frames, pairs):
    first_atom = jnp.take(frames, pairs[0], axis=2)
    second_atom = jnp.take(frames, pairs[1], axis=2)
    offset = first_atom - second_atom
    return jnp.sqrt(jnp.sum(offset * offset, axis=1) + soft_square)


def tri_solve(factor, rhs, transposed):
    return lax.linalg.triangular_solve(
        factor, rhs, left_side=True, lower=True, transpose_a=transposed
    )


def cross_gram(left_rows, right_rows):
    return lax.dot_general(
        left_rows,
        right_rows,
        (((0,), (0,)), ((), ())),
        precision=exact_mode,
        preferred_element_type=jnp.float32,
    )


def row_sum(weights, matrix):
    return jnp.dot(weights, matrix, precision=exact_mode, preferred_element_type=jnp.float32)


def subspace(c_zero, c_lag, basis_width):
    lower_factor = jnp.linalg.cholesky(c_zero)
    identity = jnp.eye(c_zero.shape[0], dtype=jnp.float32)
    basis_q = identity[:, :basis_width]
    for sweep in range(ITERS):
        inner_solve = tri_solve(lower_factor, basis_q, True)
        moved_block = jnp.dot(
            c_lag, inner_solve, precision=exact_mode, preferred_element_type=jnp.float32
        )
        image_block = tri_solve(lower_factor, moved_block, False) + spectral_shift * basis_q
        gram_small = cross_gram(image_block, image_block)
        small_factor = jnp.linalg.cholesky(gram_small)
        basis_q = tri_solve(small_factor, image_block.T, False).T
    return tri_solve(lower_factor, basis_q, True)


def on_device(coords, pairs, lengths):
    frames = coords[0]
    frame_rows = frames.shape[0]
    features = featurize(frames, pairs)
    feature_count = features.shape[1]
    frame_index = lax.axis_index("seg") * frame_rows + jnp.arange(frame_rows, dtype=jnp.int32)
    length = lengths[0]
    is_valid = (frame_index < length).astype(jnp.float32)
    paired = (frame_index + LAG < length).astype(jnp.float32)
    arriving = from_behind(features[:LAG], "seg", -1)
    lagged = jnp.concatenate([features[LAG:], arriving], axis=0)
    count_all = jnp.sum(is_valid)
    count_pair = jnp.sum(paired)
    sum_all = row_sum(is_valid, features)
    sum_lead = row_sum(paired, features)
    sum_ahead = row_sum(paired, lagged)
    own_counts = jnp.stack([count_all, count_pair])[None, :]
    own_totals = jnp.stack([sum_all, sum_lead, sum_ahead])[None]
    all_counts, all_totals = (
        lax.all_gather(own_counts, ("traj", "seg"), axis=0, tiled=True),
        lax.all_gather(own_totals, ("traj", "seg"), axis=0, tiled=True),
    )
    frames_total = jnp.sum(all_counts[:, 0])
    pairs_total = jnp.sum(all_counts[:, 1])
    mean_all = jnp.sum(all_totals[:, 0], axis=0) / frames_total
    mean_lead = jnp.sum(all_totals[:, 1], axis=0) / pairs_total
    mean_ahead = jnp.sum(all_totals[:, 2], axis=0) / pairs_total
    center_all = sum_all / jnp.maximum(count_all, 1.0)
    center_lead = sum_lead / jnp.maximum(count_pair, 1.0)
    center_ahead = sum_ahead / jnp.maximum(count_pair, 1.0)
    centered = (features - center_all) * is_valid[:, None]
    lead_rows = (features - center_lead) * paired[:, None]
    ahead_rows = (lagged - center_ahead) * paired[:, None]
    gram_zero = cross_gram(centered, centered)
    gram_lag = cross_gram(lead_rows, ahead_rows)
    total_zero, total_lag = lax.psum((gram_zero, gram_lag), ("traj", "seg"))
    symmetric_lag = total_lag + total_lag.T
    safe_counts = jnp.maximum(all_counts, 1.0)
    spread_all = all_totals[:, 0] / safe_counts[:, 0:1] - mean_all
    spread_lead = all_totals[:, 1] / safe_counts[:, 1:2] - mean_lead
    spread_ahead = all_totals[:, 2] / safe_counts[:, 1:2] - mean_ahead
    total_zero = total_zero + cross_gram(spread_all * all_counts[:, 0:1], spread_all)
    between_lag = cross_gram(spread_lead * all_counts[:, 1:2], spread_ahead)
    symmetric_lag = symmetric_lag + between_lag + between_lag.T
    identity = jnp.eye(feature_count, dtype=jnp.float32)
    c_zero = total_zero / frames_total + ridge_term * identity
    c_lag = symmetric_lag / (2.0 * pairs_total)
    basis = subspace(c_zero, c_lag, K)
    shifted = (features - mean_all) * is_valid[:, None]
    projected = jnp.dot(shifted, basis, precision=exact_mode, preferred_element_type=jnp.float32)
    return projected[None]


def solution(mesh):
    return jax.shard_map(
        on_device,
        mesh=mesh,
        in_specs=(P("traj", "seg", None, None), P(), P("traj")),
        out_specs=P("traj", "seg", None),
        check_vma=False,
    )
```

profile of v0, /device:TPU:1, one launch (start us, length us, event | category | flops | bytes accessed | tf_op | source)
XLA Modules:
  0.0 1033.5 jit_solution(3482435308951660966)
XLA Ops:
  8.9 3.6 gather_fusion
  12.5 8.0 gather_fusion.1
  20.4 7.7 fusion.4
  28.3 5.1 collective-permute-start
  37.6 5.6 fusion.27
  43.9 5.6 fusion.22
  51.7 80.3 %all-reduce.1 = f32[512]{0:T(512)S(1)} all-reduce(f32[512]{0:T(512)S(1)} %maximum_dynamic-update-slice_fusion), channel_id=3, replica_groups=mesh['traj'=32,'seg'=8] {'traj','seg'}, use_global_device_ids=true, to_apply=%add.1 | all-reduce | flops 512 | bytes 4096
  136.0 193.8 %all-reduce.5.cloned.1.call-done = (f32[1024,1024]{1,0:T(8,128)}, f32[1024,1024]{0,1:T(8,128)}) async-done(((f32[1024,1024]{1,0:T(8,128)}, f32[1024,1024]{0,1:T(8,128)}), (f32[1024,1024]{1,0:T(8,128)}, f32[1024,1024]{0,1:T(8,128)})) %all-reduce.5.cloned.1.call-update) | async-done | bytes 8388624 | tf_op jit(solution)/shard_map/psum | solution.py:99
  329.7 5.3 copy.134
  335.1 115.0 %all-gather.5.cloned.1.call-done = f32[256,3,1024]{2,1,0:T(4,128)} async-done(((f32[1,3,1024]{2,1,0:T(4,128)}), f32[256,3,1024]{2,1,0:T(4,128)}) %all-gather.5.cloned.1.call-update) | async-done | bytes 3145744 | tf_op jit(solution)/shard_map/all_gather | solution.py:84
  450.1 6.1 slice_reduce_fusion.2
  457.8 9.7 broadcast_multiply_fusion
  467.5 6.7 select_add_fusion
  474.1 5.5 copy.116
  479.7 4.4 fusion.2
  484.1 2.0 copy-done.3
  486.1 11.7 %cholesky.236 = f32[128,128]{1,0:T(8,128)S(1)} custom-call(f32[128,128]{1,0:T(8,128)S(1)} %cholesky.667), custom_call_target="Cholesky" | custom-call | tf_op jit(solution)/shard_map/jit(cholesky)/cholesky | solution.py:49
  497.8 9.8 custom-call.70
  511.5 11.7 %cholesky.259 = f32[128,128]{1,0:T(8,128)S(1)} custom-call(f32[128,128]{1,0:T(8,128)S(1)} %cholesky.671), custom_call_target="Cholesky" | custom-call | tf_op jit(solution)/shard_map/jit(cholesky)/cholesky | solution.py:49
  524.6 2.5 cholesky.266
  527.1 9.8 custom-call.71
  538.5 2.3 convolution_dynamic-update-slice_fusion
  540.8 2.7 convolution_subtract_fusion.1
  543.5 11.7 %cholesky.493 = f32[128,128]{1,0:T(8,128)S(1)} custom-call(f32[128,128]{1,0:T(8,128)S(1)} %cholesky.676), custom_call_target="Cholesky" | custom-call | tf_op jit(solution)/shard_map/jit(cholesky)/cholesky | solution.py:49
  556.0 9.8 custom-call.72
  567.0 3.5 convolution_subtract_fusion.2
  570.6 11.7 %cholesky.512 = f32[128,128]{1,0:T(8,128)S(1)} custom-call(f32[128,128]{1,0:T(8,128)S(1)} %cholesky.681), custom_call_target="Cholesky" | custom-call | tf_op jit(solution)/shard_map/jit(cholesky)/cholesky | solution.py:49
  583.1 9.8 custom-call.73
  594.0 3.2 convolution_subtract_fusion.3
  597.2 11.9 %cholesky.531 = f32[128,128]{1,0:T(8,128)S(1)} custom-call(f32[128,128]{1,0:T(8,128)S(1)} %cholesky.686), custom_call_target="Cholesky" | custom-call | tf_op jit(solution)/shard_map/jit(cholesky)/cholesky | solution.py:49
  609.8 9.8 custom-call.74
  620.8 3.1 convolution_subtract_fusion.4
  623.9 11.7 %cholesky.551 = f32[128,128]{1,0:T(8,128)S(1)} custom-call(f32[128,128]{1,0:T(8,128)S(1)} %cholesky.691), custom_call_target="Cholesky" | custom-call | tf_op jit(solution)/shard_map/jit(cholesky)/cholesky | solution.py:49
  636.3 9.8 custom-call.75
  647.1 2.9 convolution_subtract_fusion.5
  650.0 11.7 %cholesky.571 = f32[128,128]{1,0:T(8,128)S(1)} custom-call(f32[128,128]{1,0:T(8,128)S(1)} %cholesky.696), custom_call_target="Cholesky" | custom-call | tf_op jit(solution)/shard_map/jit(cholesky)/cholesky | solution.py:49
  662.5 9.8 custom-call.76
  673.3 2.1 convolution_subtract_fusion.41
  675.3 11.7 %cholesky.589 = f32[128,128]{1,0:T(8,128)S(1)} custom-call(f32[128,128]{1,0:T(8,128)S(1)} %convolution_subtract_fusion.41), custom_call_target="Cholesky" | custom-call | tf_op jit(solution)/shard_map/jit(cholesky)/cholesky | solution.py:49
  697.9 4.9 select_select_fusion
  702.8 28.7 %while.14 = (s32[]{:T(128)}, f32[1024,1024]{0,1:T(8,128)}, s32[8,2]{0,1:T(2,128)S(1)}, f32[8,128,128]{2,1,0:T(8,128)}, s32[]{:T(128)}) while((s32[]{:T(128)}, f32[1024,1024]{0,1:T(8,128)}, s32[8,2]{0,1:T(2,128)S(1)}, f32[8,128,128]{2,1,0:T(8,128)}, s32[]{:T(128)}) %tuple.152), condition=%wide.while_cond.clone.2, body=%wide.while_body.clone.2.sunk | while | flops 2 | bytes 393829 | solution.py:29
  703.4 2.3 dynamic-slice.20
  707.0 2.3 dynamic-slice.20
  710.6 2.3 dynamic-slice.20
  714.2 2.3 dynamic-slice.20
  717.8 2.3 dynamic-slice.20
  721.4 2.3 dynamic-slice.20
  724.9 2.3 dynamic-slice.20
  728.5 2.2 dynamic-slice.20
  731.5 79.8 %custom-call.93 = f32[8,128,128]{1,2,0:T(8,128)S(1)} custom-call(f32[8,128,128]{2,1,0:T(8,128)} %get-tuple-element.62), custom_call_target="InvertDiagBlocksLowerTriangular" | custom-call | tf_op jit(solution)/shard_map/triangular_solve/custom-call.16 | solution.py:29
  823.1 1.9 convolution_subtract_fusion.36
  826.3 5.2 fusion.6
  831.5 5.5 copy.135
  837.0 7.9 fusion
  846.9 3.4 fusion.333
  866.1 11.7 %cholesky.636 = f32[128,128]{1,0:T(8,128)S(1)} custom-call(f32[128,128]{1,0:T(8,128)S(1)} %fusion.231), custom_call_target="Cholesky" | custom-call | tf_op jit(solution)/shard_map/jit(cholesky)/cholesky | solution.py:59
  879.2 9.8 custom-call.86
  904.0 3.8 fusion.334
  923.9 11.9 %cholesky.647 = f32[128,128]{1,0:T(8,128)S(1)} custom-call(f32[128,128]{1,0:T(8,128)S(1)} %fusion.229), custom_call_target="Cholesky" | custom-call | tf_op jit(solution)/shard_map/jit(cholesky)/cholesky | solution.py:59
  937.1 9.8 custom-call.89
  961.1 3.7 fusion.335
  969.7 2.2 convolution_subtract_fusion.44
  987.3 11.7 %cholesky.658 = f32[128,128]{1,0:T(8,128)S(1)} custom-call(f32[128,128]{1,0:T(8,128)S(1)} %fusion.227), custom_call_target="Cholesky" | custom-call | tf_op jit(solution)/shard_map/jit(cholesky)/cholesky | solution.py:59
  1000.3 10.0 custom-call.92
  (393 shorter events, 159.9 us)
Async XLA Ops:
  6.5 323.2 %all-reduce.5.cloned.1.call-start = ((), (), s32[]{:S(2)}) async-start(), calls=%async_computation.1 | async-start | bytes 16777216 | tf_op jit(solution)/shard_map/psum | solution.py:99
  28.3 15.2 %collective-permute-start = (f32[10,1024]{0,1:T(8,128)S(1)}, f32[10,1024]{0,1:T(8,128)S(1)}, u32[]{:S(2)}, u32[]{:S(2)}) collective-permute-start(f32[10,1024]{0,1:T(8,128)S(1)} %bitcast.438), channel_id=1, source_target_pairs={{1,0},{2,1},{3,2},{4,3},{5,4},{6,5},{7,6},{9,8},{10,9},{11,10},{12... | collective-permute-start | bytes 122888 | tf_op jit(solution)/shard_map/ppermute | solution.py:18
  49.6 400.6 %all-gather.5.cloned.1.call-start = ((), (), s32[]{:S(2)}) async-start(), calls=%async_computation | async-start | bytes 4210688 | tf_op jit(solution)/shard_map/all_gather | solution.py:84
  134.1 1.0 copy-start.6
  456.2 11.3 %copy-start.11 = (f32[1024,1024]{0,1:T(8,128)S(1)}, f32[1024,1024]{0,1:T(8,128)}, u32[]{:S(2)}) copy-start(f32[1024,1024]{0,1:T(8,128)} %get-tuple-element.165) | copy-start | bytes 12582916
  484.1 2.0 copy-start.3
  510.7 0.8 copy-start.5
  524.4 12.6 %copy-start.4 = (f32[896,128]{0,1:T(8,128)S(1)}, f32[896,128]{0,1:T(8,128)}, u32[]{:S(2)}) copy-start(f32[896,128]{0,1:T(8,128)} %copy.118) | copy-start | bytes 1376260
  825.5 0.8 copy-start.7
  837.0 9.9 copy-start.8
  844.9 1.9 copy-start
  893.4 10.5 %copy-start.1 = (f32[1024,1024]{1,0:T(8,128)S(1)}, f32[1024,1024]{1,0:T(8,128)}, u32[]{:S(2)}) copy-start(f32[1024,1024]{1,0:T(8,128)} %copy-done) | copy-start | bytes 12582916
  912.8 0.7 copy-start.9
  950.5 10.5 %copy-start.2 = (f32[1024,1024]{1,0:T(8,128)S(1)}, f32[1024,1024]{1,0:T(8,128)}, u32[]{:S(2)}) copy-start(f32[1024,1024]{1,0:T(8,128)} %copy-done) | copy-start | bytes 12582916
  972.6 13.6 %copy-start.10 = (f32[128,128]{0,1:T(8,128)S(1)}, f32[128,128]{0,1:T(8,128)}, u32[]{:S(2)}) copy-start(f32[128,128]{0,1:T(8,128)} %copy.183) | copy-start | bytes 196612
Sparse Core Ops, SparseCore 0:
  49.7 280.0 all-reduce.4
  333.3 116.7 all-gather.4
where the time goes:
time: 1040 us; the launch traced here: 1030 us
  other arithmetic  364 us (35%)
  waiting for transfers between devices  309 us (30%)
  matrix products  166 us (16%)
  local copies, waits for them, and re-layouts  85.1 us (8%)
  blocking collectives  80.3 us (8%)
  between operations  23.4 us (2%)
    psum x1, waiting for transfers between devices, on_device(): total_zero, total_lag = lax.psum((gram_zero, gram_lag), ('traj', 'seg'))  194 us
    another operation x31, other arithmetic, subspace(): lower_factor = jnp.linalg.cholesky(c_zero)  168 us
    another operation x10, other arithmetic, tri_solve(): lax.linalg.triangular_solve(factor, rhs, left_side=True, lower=True, tran...  116 us
    all_gather x1, waiting for transfers between devices, on_device(): lax.all_gather(own_totals, ('traj', 'seg'), axis=0, tiled=True)  115 us
    another operation x108, matrix products, tri_solve(): lax.linalg.triangular_solve(factor, rhs, left_side=True, lower=True, tran...  97.6 us
    unnamed x1, blocking collectives  80.3 us
    another operation x9, other arithmetic, subspace(): small_factor = jnp.linalg.cholesky(gram_small)  37.3 us
    another operation x78, local copies, waits for them, and re-layouts, tri_solve(): lax.linalg.triangular_solve(factor, rhs, left_side=True, lower=True, tran...  34 us
  transfers between devices with their start and end apart: 3, of which 2 were waited for; matrix products, arithmetic and copies ran while one was open for 2% of the time, Pallas kernels for 0%

commit v1 on v0

--- a/solution.py
+++ b/solution.py
@@ -96,7 +96,7 @@
     ahead_rows = (lagged - center_ahead) * paired[:, None]
     gram_zero = cross_gram(centered, centered)
     gram_lag = cross_gram(lead_rows, ahead_rows)
-    total_zero, total_lag = lax.psum((gram_zero, gram_lag), ("traj", "seg"))
+    total_zero, total_lag = lax.psum(lax.psum((gram_zero, gram_lag), "traj"), "seg")
     symmetric_lag = total_lag + total_lag.T
     safe_counts = jnp.maximum(all_counts, 1.0)
     spread_all = all_totals[:, 0] / safe_counts[:, 0:1] - mean_all

time: 1040 us -> 956 us (0.919)
  waiting for transfers between devices: 309 us -> 210 us
    all_gather x1, waiting for transfers between devices: 115 us -> 0.03 us  [on_device(): lax.all_gather(own_totals, ('traj', 'seg'), axis=0, tiled=True)]
    psum x1 -> x2, waiting for transfers between devices: 194 us -> 210 us  [the longest x1 128 us: on_device(): lax.psum((gram_zero, gram_lag), 'traj')]
  transfers between devices with their start and end apart: 3 -> 4, of which waited for: 2 -> 2; matrix products, arithmetic and copies ran while one was open for 2% -> 4% of each run, Pallas kernels for 0% -> 0%
where the time goes in v1:
time: 956 us; the launch traced here: 947 us
  other arithmetic  366 us (38%)
  waiting for transfers between devices  210 us (22%)
  matrix products  169 us (18%)
  local copies, waits for them, and re-layouts  89.9 us (9%)
  blocking collectives  82 us (9%)
  between operations  24.7 us (3%)
    another operation x31, other arithmetic, subspace(): lower_factor = jnp.linalg.cholesky(c_zero)  170 us
    psum x1, waiting for transfers between devices, on_device(): lax.psum((gram_zero, gram_lag), 'traj')  128 us
    another operation x10, other arithmetic, tri_solve(): lax.linalg.triangular_solve(factor, rhs, left_side=True, lower=True, tran...  116 us
    another operation x108, matrix products, tri_solve(): lax.linalg.triangular_solve(factor, rhs, left_side=True, lower=True, tran...  99.4 us
    psum x1, waiting for transfers between devices, on_device(): lax.psum(lax.psum((gram_zero, gram_lag), 'traj'), 'seg')  82.2 us
    unnamed x1, blocking collectives  82 us
    another operation x9, other arithmetic, subspace(): small_factor = jnp.linalg.cholesky(gram_small)  37.3 us
    another operation x78, local copies, waits for them, and re-layouts, tri_solve(): lax.linalg.triangular_solve(factor, rhs, left_side=True, lower=True, tran...  35.1 us
  transfers between devices with their start and end apart: 4, of which 2 were waited for; matrix products, arithmetic and copies ran while one was open for 4% of the time, Pallas kernels for 0%

profile of v1, /device:TPU:1, one launch (start us, length us, event | category | flops | bytes accessed | tf_op | source)
XLA Modules:
  0.0 947.1 jit_solution(4647347559392322370)
XLA Ops:
  9.7 8.0 gather_fusion
  17.7 8.0 gather_fusion.1
  25.7 8.5 fusion.4
  34.3 5.1 collective-permute-start
  43.7 5.6 fusion.27
  50.0 5.6 fusion.22
  57.8 82.0 %all-reduce.1 = f32[512]{0:T(512)S(1)} all-reduce(f32[512]{0:T(512)S(1)} %maximum_dynamic-update-slice_fusion), channel_id=3, replica_groups=mesh['traj'=32,'seg'=8] {'traj','seg'}, use_global_device_ids=true, to_apply=%add.1 | all-reduce | flops 512 | bytes 4096
  142.4 128.1 %all-reduce.7.cloned.1.call-done = (f32[1024,1024]{1,0:T(8,128)}, f32[1024,1024]{0,1:T(8,128)}) async-done(((f32[1024,1024]{1,0:T(8,128)}, f32[1024,1024]{0,1:T(8,128)}), (f32[1024,1024]{1,0:T(8,128)}, f32[1024,1024]{0,1:T(8,128)})) %all-reduce.7.cloned.1.call-update) | async-done | bytes 8388624 | tf_op jit(solution)/shard_map/psum | solution.py:99
  270.6 6.0 slice_reduce_fusion.2
  277.9 9.9 %broadcast_multiply_fusion = (f32[256,1,1024]{2,1,0:T(1,128)}, f32[256,1,1024]{2,1,0:T(1,128)}, f32[256,1,1024]{2,1,0:T(1,128)S(1)}, f32[256,1,1024]{2,1,0:T(1,128)S(1)}) fusion(f32[256]{0:T(256)S(1)} %get-tuple-element.150, f32[1024]{0:T(1024)S(1)} %broadcast_divide_fusion.5, f32[256]{0:T(256)S(1)} %get-tuple-element.154, ...), kind=kLoop, calls=%fused_computation.110 | loop fusion | flops 2097152 | bytes 7356416 | tf_op jit(solution)/shard_map/mul | solution.py:105
  287.8 5.2 fusion.6
  293.0 5.4 copy.135
  298.4 82.2 %all-reduce.9.cloned.1.call-done = (f32[1024,1024]{1,0:T(8,128)}, f32[1024,1024]{0,1:T(8,128)}) async-done(((f32[1024,1024]{1,0:T(8,128)}, f32[1024,1024]{0,1:T(8,128)}), (f32[1024,1024]{1,0:T(8,128)}, f32[1024,1024]{0,1:T(8,128)})) %all-reduce.9.cloned.1.call-update) | async-done | bytes 8388624 | tf_op jit(solution)/shard_map/psum | solution.py:99
  380.6 9.3 select_add_fusion
  389.9 5.5 copy.116
  395.4 4.4 fusion.2
  399.9 1.9 copy-done.3
  401.9 11.7 %cholesky.236 = f32[128,128]{1,0:T(8,128)S(1)} custom-call(f32[128,128]{1,0:T(8,128)S(1)} %cholesky.667), custom_call_target="Cholesky" | custom-call | tf_op jit(solution)/shard_map/jit(cholesky)/cholesky | solution.py:49
  413.6 9.8 %custom-call.70 = f32[1,128,128]{1,2,0:T(8,128)S(1)} custom-call(f32[1,128,128]{2,1,0:T(8,128)S(1)} %get-tuple-element.244), custom_call_target="InvertDiagBlocksLowerTriangular" | custom-call | tf_op jit(solution)/shard_map/jit(cholesky)/cholesky | solution.py:49
  426.5 11.7 %cholesky.259 = f32[128,128]{1,0:T(8,128)S(1)} custom-call(f32[128,128]{1,0:T(8,128)S(1)} %cholesky.671), custom_call_target="Cholesky" | custom-call | tf_op jit(solution)/shard_map/jit(cholesky)/cholesky | solution.py:49
  440.3 2.5 cholesky.266
  442.8 10.6 %custom-call.71 = f32[1,128,128]{1,2,0:T(8,128)S(1)} custom-call(f32[1,128,128]{2,1,0:T(8,128)} %get-tuple-element.242), custom_call_target="InvertDiagBlocksLowerTriangular" | custom-call | tf_op jit(solution)/shard_map/jit(cholesky)/cholesky | solution.py:49
  456.2 2.7 convolution_subtract_fusion.1
  458.9 11.7 %cholesky.493 = f32[128,128]{1,0:T(8,128)S(1)} custom-call(f32[128,128]{1,0:T(8,128)S(1)} %cholesky.676), custom_call_target="Cholesky" | custom-call | tf_op jit(solution)/shard_map/jit(cholesky)/cholesky | solution.py:49
  471.4 9.8 %custom-call.72 = f32[1,128,128]{1,2,0:T(8,128)S(1)} custom-call(f32[1,128,128]{2,1,0:T(8,128)S(1)} %get-tuple-element.240), custom_call_target="InvertDiagBlocksLowerTriangular" | custom-call | tf_op jit(solution)/shard_map/jit(cholesky)/cholesky | solution.py:49
  482.4 3.3 convolution_subtract_fusion.2
  485.7 11.7 %cholesky.512 = f32[128,128]{1,0:T(8,128)S(1)} custom-call(f32[128,128]{1,0:T(8,128)S(1)} %cholesky.681), custom_call_target="Cholesky" | custom-call | tf_op jit(solution)/shard_map/jit(cholesky)/cholesky | solution.py:49
  498.2 9.8 %custom-call.73 = f32[1,128,128]{1,2,0:T(8,128)S(1)} custom-call(f32[1,128,128]{2,1,0:T(8,128)S(1)} %get-tuple-element.238), custom_call_target="InvertDiagBlocksLowerTriangular" | custom-call | tf_op jit(solution)/shard_map/jit(cholesky)/cholesky | solution.py:49
  509.2 3.2 convolution_subtract_fusion.3
  512.3 11.9 %cholesky.531 = f32[128,128]{1,0:T(8,128)S(1)} custom-call(f32[128,128]{1,0:T(8,128)S(1)} %cholesky.686), custom_call_target="Cholesky" | custom-call | tf_op jit(solution)/shard_map/jit(cholesky)/cholesky | solution.py:49
  525.0 9.8 %custom-call.74 = f32[1,128,128]{1,2,0:T(8,128)S(1)} custom-call(f32[1,128,128]{2,1,0:T(8,128)S(1)} %get-tuple-element.236), custom_call_target="InvertDiagBlocksLowerTriangular" | custom-call | tf_op jit(solution)/shard_map/jit(cholesky)/cholesky | solution.py:49
  535.9 3.1 convolution_subtract_fusion.4
  539.0 11.7 %cholesky.551 = f32[128,128]{1,0:T(8,128)S(1)} custom-call(f32[128,128]{1,0:T(8,128)S(1)} %cholesky.691), custom_call_target="Cholesky" | custom-call | tf_op jit(solution)/shard_map/jit(cholesky)/cholesky | solution.py:49
  551.5 9.8 %custom-call.75 = f32[1,128,128]{1,2,0:T(8,128)S(1)} custom-call(f32[1,128,128]{2,1,0:T(8,128)S(1)} %get-tuple-element.234), custom_call_target="InvertDiagBlocksLowerTriangular" | custom-call | tf_op jit(solution)/shard_map/jit(cholesky)/cholesky | solution.py:49
  562.3 3.1 convolution_subtract_fusion.5
  565.4 11.7 %cholesky.571 = f32[128,128]{1,0:T(8,128)S(1)} custom-call(f32[128,128]{1,0:T(8,128)S(1)} %cholesky.696), custom_call_target="Cholesky" | custom-call | tf_op jit(solution)/shard_map/jit(cholesky)/cholesky | solution.py:49
  577.9 9.8 %custom-call.76 = f32[1,128,128]{1,2,0:T(8,128)S(1)} custom-call(f32[1,128,128]{2,1,0:T(8,128)S(1)} %get-tuple-element.232), custom_call_target="InvertDiagBlocksLowerTriangular" | custom-call | tf_op jit(solution)/shard_map/jit(cholesky)/cholesky | solution.py:49
  588.6 2.1 convolution_subtract_fusion.41
  590.7 11.7 %cholesky.589 = f32[128,128]{1,0:T(8,128)S(1)} custom-call(f32[128,128]{1,0:T(8,128)S(1)} %convolution_subtract_fusion.41), custom_call_target="Cholesky" | custom-call | tf_op jit(solution)/shard_map/jit(cholesky)/cholesky | solution.py:49
  613.6 4.9 select_select_fusion
  618.5 28.2 %while.14 = (s32[]{:T(128)}, f32[1024,1024]{0,1:T(8,128)}, s32[8,2]{0,1:T(2,128)S(1)}, f32[8,128,128]{2,1,0:T(8,128)}, s32[]{:T(128)}) while((s32[]{:T(128)}, f32[1024,1024]{0,1:T(8,128)}, s32[8,2]{0,1:T(2,128)S(1)}, f32[8,128,128]{2,1,0:T(8,128)}, s32[]{:T(128)}) %tuple.152), condition=%wide.while_cond.clone.2, body=%wide.while_body.clone.2.sunk | while | flops 2 | bytes 393829 | solution.py:29
  619.1 2.2 dynamic-slice.20
  622.6 2.2 dynamic-slice.20
  626.1 2.2 dynamic-slice.20
  629.6 2.2 dynamic-slice.20
  633.2 2.2 dynamic-slice.20
  636.7 2.2 dynamic-slice.20
  640.2 2.2 dynamic-slice.20
  643.8 2.1 dynamic-slice.20
  646.6 79.5 %custom-call.93 = f32[8,128,128]{1,2,0:T(8,128)S(1)} custom-call(f32[8,128,128]{2,1,0:T(8,128)} %get-tuple-element.62), custom_call_target="InvertDiagBlocksLowerTriangular" | custom-call | tf_op jit(solution)/shard_map/triangular_solve/custom-call.16 | solution.py:29
  739.5 5.5 copy.134
  745.0 7.9 fusion
  754.8 3.4 fusion.333
  764.8 2.2 convolution_subtract_fusion.52
  780.2 11.7 %cholesky.636 = f32[128,128]{1,0:T(8,128)S(1)} custom-call(f32[128,128]{1,0:T(8,128)S(1)} %fusion.231), custom_call_target="Cholesky" | custom-call | tf_op jit(solution)/shard_map/jit(cholesky)/cholesky | solution.py:59
  793.3 9.8 %custom-call.86 = f32[1,128,128]{1,2,0:T(8,128)S(1)} custom-call(f32[1,128,128]{2,1,0:T(8,128)S(1)} %fusion.207), custom_call_target="InvertDiagBlocksLowerTriangular" | custom-call | tf_op jit(solution)/shard_map/triangular_solve/custom-call.18 | solution.py:29
  817.4 3.4 fusion.334
  836.9 11.9 %cholesky.647 = f32[128,128]{1,0:T(8,128)S(1)} custom-call(f32[128,128]{1,0:T(8,128)S(1)} %fusion.229), custom_call_target="Cholesky" | custom-call | tf_op jit(solution)/shard_map/jit(cholesky)/cholesky | solution.py:59
  850.2 9.8 %custom-call.89 = f32[1,128,128]{1,2,0:T(8,128)S(1)} custom-call(f32[1,128,128]{2,1,0:T(8,128)S(1)} %fusion.208), custom_call_target="InvertDiagBlocksLowerTriangular" | custom-call | tf_op jit(solution)/shard_map/triangular_solve/custom-call.18 | solution.py:29
  871.8 1.9 convolution_subtract_fusion.16
  874.1 3.9 fusion.335
  883.0 2.2 convolution_subtract_fusion.44
  900.5 11.7 %cholesky.658 = f32[128,128]{1,0:T(8,128)S(1)} custom-call(f32[128,128]{1,0:T(8,128)S(1)} %fusion.227), custom_call_target="Cholesky" | custom-call | tf_op jit(solution)/shard_map/jit(cholesky)/cholesky | solution.py:59
  913.6 9.9 %custom-call.92 = f32[1,128,128]{1,2,0:T(8,128)S(1)} custom-call(f32[1,128,128]{2,1,0:T(8,128)S(1)} %fusion.209), custom_call_target="InvertDiagBlocksLowerTriangular" | custom-call | tf_op jit(solution)/shard_map/triangular_solve/custom-call.18 | solution.py:29
  (392 shorter events, 161.0 us)
Async XLA Ops:
  7.4 263.2 %all-reduce.7.cloned.1.call-start = ((), (), s32[]{:S(2)}) async-start(), calls=%async_computation.1 | async-start | bytes 16777216 | tf_op jit(solution)/shard_map/psum | solution.py:99
  34.3 15.2 %collective-permute-start = (f32[10,1024]{0,1:T(8,128)S(1)}, f32[10,1024]{0,1:T(8,128)S(1)}, u32[]{:S(2)}, u32[]{:S(2)}) collective-permute-start(f32[10,1024]{0,1:T(8,128)S(1)} %bitcast.438), channel_id=1, source_target_pairs={{1,0},{2,1},{3,2},{4,3},{5,4},{6,5},{7,6},{9,8},{10,9},{11,10},{12... | collective-permute-start | bytes 122888 | tf_op jit(solution)/shard_map/ppermute | solution.py:18
  55.6 215.0 %all-gather.5.cloned.1.call-start = ((), (), s32[]{:S(2)}) async-start(), calls=%async_computation | async-start | bytes 4210688 | tf_op jit(solution)/shard_map/all_gather | solution.py:84
  56.3 324.3 %all-reduce.9.cloned.1.call-start = ((), (), s32[]{:S(2)}) async-start(), calls=%async_computation.2 | async-start | bytes 16777216 | tf_op jit(solution)/shard_map/psum | solution.py:99
  399.9 2.0 copy-start.3
  439.8 14.4 %copy-start.8 = (f32[128,128]{0,1:T(8,128)S(1)}, f32[128,128]{0,1:T(8,128)}, u32[]{:S(2)}) copy-start(f32[128,128]{0,1:T(8,128)} %copy.119) | copy-start | bytes 196612
  613.6 4.9 copy-start.9
  752.9 1.9 copy-start
  763.3 0.8 copy-start.4
  764.0 0.7 copy-start.5
  806.7 10.7 %copy-start.1 = (f32[1024,1024]{1,0:T(8,128)S(1)}, f32[1024,1024]{1,0:T(8,128)}, u32[]{:S(2)}) copy-start(f32[1024,1024]{1,0:T(8,128)} %copy-done) | copy-start | bytes 12582916
  825.9 0.7 copy-start.6
  863.6 10.5 %copy-start.2 = (f32[1024,1024]{1,0:T(8,128)S(1)}, f32[1024,1024]{1,0:T(8,128)}, u32[]{:S(2)}) copy-start(f32[1024,1024]{1,0:T(8,128)} %copy-done) | copy-start | bytes 12582916
  885.9 13.6 %copy-start.7 = (f32[128,128]{0,1:T(8,128)S(1)}, f32[128,128]{0,1:T(8,128)}, u32[]{:S(2)}) copy-start(f32[128,128]{0,1:T(8,128)} %copy.183) | copy-start | bytes 196612
Sparse Core Ops, SparseCore 0:
  55.7 214.7 all-reduce.6
  273.0 107.6 all-reduce.8
Sparse Core Ops, SparseCore 1:
  59.7 142.1 all-gather.4
